TPU v7x, 32 devices: a whole 2x2x4 slice. The times are simulated.
32 devices in a mesh: member: 4 (over x, core), space: 8 (over z, y).
Axes of the slice: x: 2, y: 2, z: 4, core: 2. Of those that a mesh axis runs over, the one named last changes fastest.
Arguments:
- features: bfloat16 [4, 641, 192, 128], P('member', None, 'space'), may hold values from -6 to 6
- depth_kernel: float32 [641, 5, 5], replicated, may hold values from -1.25 to 1.25
- in_weight: bfloat16 [641, 1282], replicated, may hold values from -0.25 to 0.25
- out_weight: bfloat16 [1282, 641], replicated, may hold values from -0.15625 to 0.15625
- decoder_weight: bfloat16 [641, 72], replicated, may hold values from -0.25 to 0.25
- observed: float32 [72, 192, 128], P(None, 'space'), may hold values from -6 to 6
- land_mask: int32 [192, 128], P('space'), may hold values 0 or 1
Outputs:
- grad_features: bfloat16 [4, 641, 192, 128], P('member', None, 'space')
- decoder_grad: float32 [641, 72], replicated
All inputs are finite; a program needn't handle non-finite values. No bound on the sum of `land_mask` on one device may be relied on, other than what follows from the above.
Results may differ from a plain program's by a relative error of at most 0.0054.
Values may be sent and summed in bfloat16 or wider, within the bound.
A program may use at most 128 MiB of HBM per device.

v0:
```python
import math
import jax
import jax.numpy as jnp
from jax import lax
from jax.sharding import PartitionSpec as P

norm_eps = 1e-05


def padded_2(cells, sides, width):
    for axis, dim in sides:
        count = lax.axis_size(axis)
        head = lax.slice_in_dim(cells, 0, width, axis=dim)
        tail = lax.slice_in_dim(cells, cells.shape[dim] - width, cells.shape[dim], axis=dim)
        cells = jnp.concatenate(
            [
                lax.ppermute(tail, axis, [(i, (i + 1) % count) for i in range(count)]),
                cells,
                lax.ppermute(head, axis, [((i + 1) % count, i) for i in range(count)]),
            ],
            axis=dim,
        )
    return cells


def per_device(features, depth_kernel, in_weight, out_weight, decoder_weight, observed, land_mask):
    channels = features.shape[1]
    lon_len = features.shape[2]
    lat_len = features.shape[3]
    points = lon_len * lat_len
    padded = padded_2(features, (("space", 2),), 2)
    widened = jnp.pad(padded.astype(jnp.float32), ((0, 0), (0, 0), (0, 0), (2, 2)))
    convolved = jnp.zeros(features.shape, jnp.float32)
    for row_off in range(5):
        for col_off in range(5):
            convolved = (
                convolved
                + depth_kernel[:, row_off, col_off][None, :, None, None]
                * widened[:, :, row_off : row_off + lon_len, col_off : col_off + lat_len]
            )
    center = jnp.mean(convolved, axis=1, keepdims=True)
    shifted = convolved - center
    normed = (
        shifted * lax.rsqrt(jnp.mean(shifted * shifted, axis=1, keepdims=True) + norm_eps)
    ).astype(jnp.bfloat16)
    flat = normed.reshape(channels, points)
    hidden = jax.nn.gelu(
        jnp.einsum("ch,cp->hp", in_weight, flat, preferred_element_type=jnp.float32),
        approximate=False,
    ).astype(jnp.bfloat16)
    mlp_out = jnp.einsum("hc,hp->cp", out_weight, hidden, preferred_element_type=jnp.float32)
    block_out = (features.reshape(channels, points).astype(jnp.float32) + mlp_out).astype(
        jnp.bfloat16
    )
    decoded_flat = jnp.einsum(
        "co,cp->op", decoder_weight, block_out, preferred_element_type=jnp.float32
    ).astype(jnp.bfloat16)
    outputs = decoded_flat.shape[0]
    decoded = decoded_flat.reshape(1, outputs, lon_len, lat_len)
    groups = lax.axis_size("member")
    members = features.shape[0] * groups
    point_weight = 4.0 + 8.0 * land_mask.astype(jnp.float32)
    own_f = decoded.astype(jnp.float32)
    apart = own_f - lax.all_gather(decoded, "member", axis=0, tiled=True).astype(jnp.float32)
    apart_norm = jnp.sqrt(jnp.sum(apart * apart, axis=1, keepdims=True) + 1.0)
    pair_sum = jnp.sum(apart / apart_norm, axis=0, keepdims=True)
    misfit = own_f - observed[None]
    misfit_norm = jnp.sqrt(jnp.sum(misfit * misfit, axis=1, keepdims=True) + 1.0)
    score_grad = (point_weight[None, None] * (misfit / misfit_norm - pair_sum / members)).astype(
        jnp.bfloat16
    )
    grad_flat = score_grad.reshape(outputs, points)
    grad_features = jnp.einsum(
        "co,op->cp", decoder_weight, grad_flat, preferred_element_type=jnp.float32
    ).astype(jnp.bfloat16)
    total_points = lon_len * lax.axis_size("space") * lat_len
    term = jnp.einsum(
        "cp,op->co", block_out, grad_flat, preferred_element_type=jnp.float32
    ) / math.sqrt(members * total_points)
    decoder_grad = lax.psum(term, ("member", "space"))
    return (grad_features.reshape(features.shape), decoder_grad)


def solution(mesh):
    placed = (
        P("member", None, "space", None),
        P(),
        P(),
        P(),
        P(),
        P(None, "space", None),
        P("space", None),
    )
    return jax.shard_map(
        per_device,
        mesh=mesh,
        in_specs=placed,
        out_specs=(P("member", None, "space", None), P()),
        check_vma=False,
    )
```

profile of v0, /device:TPU:8, one launch (start us, length us, event | category | flops | bytes accessed | tf_op | source)
XLA Modules:
  0.0 393.1 jit_solution(12034791294327075821)
XLA Ops:
  7.2 2.3 fusion.106
  9.6 1.6 collective-permute-start
  11.3 1.5 collective-permute-start.1
  12.7 2.6 convert_bitcast_fusion
  15.9 5.0 %copy.15 = f32[81,8,24,128]{3,1,2,0:T(8,128)} copy(f32[81,8,24,128]{3,2,1,0:T(8,128)S(1)} %bitcast.131) | data formatting | bytes 15925248
  21.1 4.2 %collective-permute-done = bf16[1,641,2,128]{3,1,2,0:T(8,128)(2,1)S(1)} collective-permute-done((bf16[1,641,2,128]{3,1,2,0:T(8,128)(2,1)S(1)}, bf16[1,641,2,128]{3,1,2,0:T(8,128)(2,1)S(1)}, u32[]{:S(2)}, u32[]{:S(2)}) %collective-permute-start) | collective-permute-done | bytes 328224 | tf_op jit(solution)/shard_map/ppermute | solution.py:17
  25.6 1.6 collective-permute-done.1
  27.5 6.9 %maximum_convert_fusion = f32[1,641,28,128]{3,2,1,0:T(8,128)} fusion(bf16[1,641,2,128]{3,2,1,0:T(2,128)(2,1)S(1)} %copy.12, bf16[1,641,24,128]{3,2,1,0:T(8,128)(2,1)S(1)} %copy-done.5, bf16[1,641,2,128]{3,2,1,0:T(2,128)(2,1)S(1)} %copy.11), kind=kLoop, calls=%fused_computation.100 | loop fusion | flops 13784064 | bytes 13784064 | tf_op jit(solution)/shard_map/convert_element_type | solution.py:32
  34.4 130.6 %fusion.104 = (f32[24,128]{1,0:T(8,128)S(1)}, f32[1,641,24,128]{3,2,1,0:T(8,128)}) fusion(f32[641]{0:T(1024)S(1)} %get-tuple-element.25, f32[641]{0:T(1024)S(1)} %get-tuple-element.26, f32[1,641,28,128]{3,2,1,0:T(8,128)} %maximum_convert_fusion, f32[641]{0:T(1024)S(1)} %get-tuple-element.3, f32[641]{0:T(1024)S(1)} %get-tuple-element.4, ...), kind=kLoop, calls=%fused_computation.177 | loop fusion | flops 98454528 | bytes 57838180 | tf_op jit(solution)/shard_map/reduce_sum | solution.py:41
  165.0 4.3 %multiply_reduce_fusion = f32[24,128]{1,0:T(8,128)S(1)} fusion(f32[1,641,24,128]{3,2,1,0:T(8,128)} %get-tuple-element.28, f32[24,128]{1,0:T(8,128)S(1)} %broadcast_multiply_fusion), kind=kLoop, calls=%fused_computation.99 | loop fusion | flops 5904384 | bytes 7901184 | tf_op jit(solution)/shard_map/reduce_sum | solution.py:44
  169.3 1.1 copy-done.2
  172.0 1.1 copy.16
  173.2 42.9 %fusion.123 = bf16[1282,3072]{1,0:T(8,128)(2,1)S(1)} fusion(bf16[641,3072]{1,0:T(8,128)(2,1)S(1)} %bitcast.142, bf16[641,1282]{1,0:T(8,128)(2,1)S(1)} %copy-done), kind=kOutput, calls=%fused_computation.23.clone.clone.clone.clone.1 | convolution fusion | flops 5304895488 | bytes 13458436 | tf_op jit(solution)/shard_map/ch,cp->hp/dot_general | solution.py:48
  216.2 7.2 %fusion.18 = bf16[641,3072]{1,0:T(8,128)(2,1)S(1)} fusion(f32[641,3072]{1,0:T(8,128)S(1)} %bitcast.138, bf16[1282,641]{0,1:T(8,128)(2,1)S(1)} %copy-done.10, bf16[1282,3072]{1,0:T(8,128)(2,1)S(1)} %fusion.123), kind=kOutput, calls=%fused_computation.45 | convolution fusion | flops 5052844032 | bytes 21335044 | tf_op jit(solution)/shard_map/hc,hp->cp/dot_general | solution.py:51
  223.4 1.9 copy-done.3
  227.4 20.9 %all-gather.2.cloned.1.call-done = bf16[4,72,24,128]{3,2,1,0:T(8,128)(2,1)} async-done(((bf16[1,72,24,128]{3,2,1,0:T(8,128)(2,1)}), bf16[4,72,24,128]{3,2,1,0:T(8,128)(2,1)}) %all-gather.2.cloned.1.call-update) | async-done | bytes 1769488 | tf_op jit(solution)/shard_map/all_gather | solution.py:64
  248.4 2.1 multiply_reduce_fusion.1
  250.5 2.0 divide_reduce_fusion
  252.7 2.0 convolution_multiply_fusion
  254.7 3.1 convolution_convert_fusion
  257.9 3.4 copy.20
  261.3 2.6 slice_bitcast_fusion
  263.9 120.7 %all-reduce.3.cloned.1.call-done = f32[641,72]{0,1:T(8,128)} async-done(((f32[641,72]{0,1:T(8,128)}), f32[641,72]{0,1:T(8,128)}) %all-reduce.3.cloned.1.call-update) | async-done | bytes 184624 | tf_op jit(solution)/shard_map/psum | solution.py:80
  384.6 1.6 copy.30
  (48 shorter events, 5.3 us)
Async XLA Ops:
  7.2 166.0 %copy-start = (bf16[641,1282]{1,0:T(8,128)(2,1)S(1)}, bf16[641,1282]{1,0:T(8,128)(2,1)}, u32[]{:S(2)}) copy-start(bf16[641,1282]{1,0:T(8,128)(2,1)} %param.9) | copy-start | bytes 4930576
  7.2 241.2 %all-gather.2.cloned.1.call-start = ((), (), s32[]{:S(2)}) async-start(), calls=%async_computation | async-start | bytes 2211840 | tf_op jit(solution)/shard_map/all_gather | solution.py:64
  9.6 15.7 %collective-permute-start = (bf16[1,641,2,128]{3,1,2,0:T(8,128)(2,1)S(1)}, bf16[1,641,2,128]{3,1,2,0:T(8,128)(2,1)S(1)}, u32[]{:S(2)}, u32[]{:S(2)}) collective-permute-start(bf16[1,641,2,128]{3,1,2,0:T(8,128)(2,1)S(1)} %copy.13), channel_id=1, source_target_pairs={{0,1},{1,2},{2,3},{3,4},{4,5},{5,6},{6,7},{7,0},{8,9},{9,10},{10,1... | collective-permute-start | bytes 984584 | tf_op jit(solution)/shard_map/ppermute | solution.py:17
  11.3 16.0 %collective-permute-start.1 = (bf16[1,641,2,128]{3,1,2,0:T(8,128)(2,1)S(1)}, bf16[1,641,2,128]{3,1,2,0:T(8,128)(2,1)S(1)}, u32[]{:S(2)}, u32[]{:S(2)}) collective-permute-start(bf16[1,641,2,128]{3,1,2,0:T(8,128)(2,1)S(1)} %copy.14), channel_id=1, source_target_pairs={{1,0},{2,1},{3,2},{4,3},{5,4},{6,5},{7,6},{0,7},{9,8},{10,9},{11,1... | collective-permute-start | bytes 984584 | tf_op jit(solution)/shard_map/ppermute | solution.py:19
  15.9 5.0 %copy-start.8 = (f32[641,5,5]{0,2,1:T(8,128)S(1)}, f32[641,5,5]{0,2,1:T(8,128)}, u32[]{:S(2)}) copy-start(f32[641,5,5]{0,2,1:T(8,128)} %param.8) | copy-start | bytes 192304
  15.9 11.6 %copy-start.5 = (bf16[1,641,24,128]{3,2,1,0:T(8,128)(2,1)S(1)}, bf16[1,641,24,128]{3,2,1,0:T(8,128)(2,1)}, u32[]{:S(2)}) copy-start(bf16[1,641,24,128]{3,2,1,0:T(8,128)(2,1)} %param.7) | copy-start | bytes 11814916
  164.9 5.5 %copy-start.2 = (f32[1,641,24,128]{3,2,1,0:T(8,128)S(1)}, f32[1,641,24,128]{3,2,1,0:T(8,128)}, u32[]{:S(2)}) copy-start(f32[1,641,24,128]{3,2,1,0:T(8,128)} %get-tuple-element.28) | copy-start | bytes 23629828
  172.0 44.1 %slice-start = ((s8[7962624]{0:T(1024)(128)(4,1)}), s8[4194304]{0:T(1024)(128)(4,1)S(1)}, s32[]{:S(2)}) async-start(s8[7962624]{0:T(1024)(128)(4,1)} %bitcast.136), calls=%async_computation.2 | async-start | bytes 8388608
  173.1 43.0 %slice-start.1 = ((s8[7962624]{0:T(1024)(128)(4,1)}), s8[3768320]{0:T(1024)(128)(4,1)S(1)}, s32[]{:S(2)}) async-start(s8[7962624]{0:T(1024)(128)(4,1)} %bitcast.136), calls=%async_computation.3 | async-start | bytes 7536640
  173.2 43.0 %copy-start.10 = (bf16[1282,641]{0,1:T(8,128)(2,1)S(1)}, bf16[1282,641]{0,1:T(8,128)(2,1)}, u32[]{:S(2)}) copy-start(bf16[1282,641]{0,1:T(8,128)(2,1)} %param.10) | copy-start | bytes 4930576
  216.1 9.1 %copy-start.7 = (bf16[641,72]{0,1:T(8,128)(2,1)S(1)}, bf16[641,72]{0,1:T(8,128)(2,1)}, u32[]{:S(2)}) copy-start(bf16[641,72]{0,1:T(8,128)(2,1)} %param.11) | copy-start | bytes 276916
  223.4 1.9 copy-start.3
  225.3 1.9 copy-start.6
  225.3 2.1 copy-start.9
  226.9 157.7 %all-reduce.3.cloned.1.call-start = ((), (), s32[]{:S(2)}) async-start(), calls=%async_computation.1 | async-start | bytes 442368 | tf_op jit(solution)/shard_map/psum | solution.py:80
  248.3 4.4 %copy-start.4 = (bf16[641,3072]{1,0:T(8,128)(2,1)S(1)}, bf16[641,3072]{1,0:T(8,128)(2,1)}, u32[]{:S(2)}) copy-start(bf16[641,3072]{1,0:T(8,128)(2,1)} %copy-done.3) | copy-start | bytes 11814916
  257.9 128.3 %copy-start.1 = (bf16[641,1282]{1,0:T(8,128)(2,1)S(1)}, bf16[641,1282]{1,0:T(8,128)(2,1)}, u32[]{:S(2)}) copy-start(bf16[641,1282]{1,0:T(8,128)(2,1)} %param.9) | copy-start | bytes 4930576
Sparse Core Ops, SparseCore 0:
  227.0 21.2 all-gather.1
  258.0 126.5 all-reduce.2
where the time goes:
time: 393 us
  other arithmetic  150 us (38%)
  waiting for transfers between devices  148 us (38%)
  matrix products  56.1 us (14%)
  local copies, waits for them, and re-layouts  22.2 us (6%)
  between operations  14.3 us (4%)
    reduce_sum x1, other arithmetic, per_device(): center = jnp.mean(convolved, axis=1, keepdims=True)  131 us
    psum x1, waiting for transfers between devices, per_device(): decoder_grad = lax.psum(term, ('member', 'space'))  121 us
    dot_general x1, matrix products, per_device(): jnp.einsum('ch,cp->hp', in_weight, flat, preferred_element_type=jnp.float32)  42.9 us
    all_gather x1, waiting for transfers between devices, per_device(): lax.all_gather(decoded, 'member', axis=0, tiled=True).astype(jnp.float32)  20.9 us
    unnamed x36, local copies, waits for them, and re-layouts  16.6 us
  transfers between devices with their start and end apart: 4, of which 4 were waited for; matrix products, arithmetic and copies ran while one was open for 4% of the time, Pallas kernels for 0%

commit v1 on v0

--- a/solution.py
+++ b/solution.py
@@ -77,7 +77,8 @@
     term = jnp.einsum(
         "cp,op->co", block_out, grad_flat, preferred_element_type=jnp.float32
     ) / math.sqrt(members * total_points)
-    decoder_grad = lax.psum(term, ("member", "space"))
+    parts = lax.all_gather(term, ("member", "space"), axis=0, tiled=False)
+    decoder_grad = parts.sum(axis=0)
     return (grad_features.reshape(features.shape), decoder_grad)
 
 

time: 393 us -> 340 us (0.87)
  waiting for transfers between devices: 148 us -> 94 us
  other arithmetic: 150 us -> 154 us
    psum x1 -> x0, waiting for transfers between devices: 121 us -> none  [per_device(): decoder_grad = lax.psum(term, ('member', 'space'))]
    all_gather x0 -> x1, waiting for transfers between devices: none -> 67.1 us  [per_device(): parts = lax.all_gather(term, ('member', 'space'), axis=0, tiled=False)]
    reduce_sum x0 -> x1, other arithmetic: none -> 4.07 us  [per_device(): decoder_grad = parts.sum(axis=0)]
    unnamed x36 -> x35, local copies, waits for them, and re-layouts: 16.6 us -> 12.7 us
where the time goes in v1:
time: 340 us; the launch traced here: 338 us
  other arithmetic  154 us (45%)
  waiting for transfers between devices  94 us (28%)
  matrix products  54.2 us (16%)
  local copies, waits for them, and re-layouts  18.3 us (5%)
  between operations  14.3 us (4%)
    reduce_sum x1, other arithmetic, per_device(): center = jnp.mean(convolved, axis=1, keepdims=True)  131 us
    all_gather x1, waiting for transfers between devices, per_device(): parts = lax.all_gather(term, ('member', 'space'), axis=0, tiled=False)  67.1 us
    dot_general x1, matrix products, per_device(): jnp.einsum('ch,cp->hp', in_weight, flat, preferred_element_type=jnp.float32)  42.9 us
    all_gather x1, waiting for transfers between devices, per_device(): lax.all_gather(decoded, 'member', axis=0, tiled=True).astype(jnp.float32)  20.9 us
    unnamed x35, local copies, waits for them, and re-layouts  12.7 us
    dot_general x1, matrix products, per_device(): jnp.einsum('hc,hp->cp', out_weight, hidden, preferred_element_type=jnp.fl...  7.22 us
    convert_element_type x1, other arithmetic, per_device(): padded.astype(jnp.float32)  6.88 us
  transfers between devices with their start and end apart: 4, of which 4 were waited for; matrix products, arithmetic and copies ran while one was open for 4% of the time, Pallas kernels for 0%

profile of v1, /device:TPU:8, one launch (start us, length us, event | category | flops | bytes accessed | tf_op | source)
XLA Modules:
  0.0 337.8 jit_solution(8393234483265893448)
XLA Ops:
  7.2 2.3 fusion.107
  9.6 1.6 collective-permute-start
  11.3 1.5 collective-permute-start.1
  12.7 2.6 convert_bitcast_fusion
  15.9 5.0 %copy.15 = f32[81,8,24,128]{3,1,2,0:T(8,128)} copy(f32[81,8,24,128]{3,2,1,0:T(8,128)S(1)} %bitcast.133) | data formatting | bytes 15925248
  21.1 4.2 %collective-permute-done = bf16[1,641,2,128]{3,1,2,0:T(8,128)(2,1)S(1)} collective-permute-done((bf16[1,641,2,128]{3,1,2,0:T(8,128)(2,1)S(1)}, bf16[1,641,2,128]{3,1,2,0:T(8,128)(2,1)S(1)}, u32[]{:S(2)}, u32[]{:S(2)}) %collective-permute-start) | collective-permute-done | bytes 328224 | tf_op jit(solution)/shard_map/ppermute | solution.py:17
  25.6 1.6 collective-permute-done.1
  27.5 6.9 %maximum_convert_fusion = f32[1,641,28,128]{3,2,1,0:T(8,128)} fusion(bf16[1,641,2,128]{3,2,1,0:T(2,128)(2,1)S(1)} %copy.12, bf16[1,641,24,128]{3,2,1,0:T(8,128)(2,1)S(1)} %copy-done.5, bf16[1,641,2,128]{3,2,1,0:T(2,128)(2,1)S(1)} %copy.11), kind=kLoop, calls=%fused_computation.100 | loop fusion | flops 13784064 | bytes 13784064 | tf_op jit(solution)/shard_map/convert_element_type | solution.py:32
  34.4 130.5 %fusion.105 = (f32[24,128]{1,0:T(8,128)S(1)}, f32[1,641,24,128]{3,2,1,0:T(8,128)}) fusion(f32[641]{0:T(1024)S(1)} %get-tuple-element.25, f32[641]{0:T(1024)S(1)} %get-tuple-element.26, f32[1,641,28,128]{3,2,1,0:T(8,128)} %maximum_convert_fusion, f32[641]{0:T(1024)S(1)} %get-tuple-element.3, f32[641]{0:T(1024)S(1)} %get-tuple-element.4, ...), kind=kLoop, calls=%fused_computation.178 | loop fusion | flops 98454528 | bytes 57838180 | tf_op jit(solution)/shard_map/reduce_sum | solution.py:41
  164.9 4.3 %multiply_reduce_fusion = f32[24,128]{1,0:T(8,128)S(1)} fusion(f32[1,641,24,128]{3,2,1,0:T(8,128)} %get-tuple-element.28, f32[24,128]{1,0:T(8,128)S(1)} %broadcast_multiply_fusion), kind=kLoop, calls=%fused_computation.99 | loop fusion | flops 5904384 | bytes 7901184 | tf_op jit(solution)/shard_map/reduce_sum | solution.py:44
  169.2 1.1 copy-done.2
  171.9 1.2 copy.16
  173.1 42.9 %fusion.124 = bf16[1282,3072]{1,0:T(8,128)(2,1)S(1)} fusion(bf16[641,3072]{1,0:T(8,128)(2,1)S(1)} %bitcast.144, bf16[641,1282]{1,0:T(8,128)(2,1)S(1)} %copy-done), kind=kOutput, calls=%fused_computation.23.clone.clone.clone.clone.1 | convolution fusion | flops 5304895488 | bytes 13458436 | tf_op jit(solution)/shard_map/ch,cp->hp/dot_general | solution.py:48
  216.1 7.2 %fusion.18 = bf16[641,3072]{1,0:T(8,128)(2,1)S(1)} fusion(f32[641,3072]{1,0:T(8,128)S(1)} %bitcast.140, bf16[1282,641]{0,1:T(8,128)(2,1)S(1)} %copy-done.10, bf16[1282,3072]{1,0:T(8,128)(2,1)S(1)} %fusion.124), kind=kOutput, calls=%fused_computation.45 | convolution fusion | flops 5052844032 | bytes 21335044 | tf_op jit(solution)/shard_map/hc,hp->cp/dot_general | solution.py:51
  223.4 1.9 copy-done.3
  227.4 20.9 %all-gather.5.cloned.1.call-done = bf16[4,72,24,128]{3,2,1,0:T(8,128)(2,1)} async-done(((bf16[1,72,24,128]{3,2,1,0:T(8,128)(2,1)}), bf16[4,72,24,128]{3,2,1,0:T(8,128)(2,1)}) %all-gather.5.cloned.1.call-update) | async-done | bytes 1769488 | tf_op jit(solution)/shard_map/all_gather | solution.py:64
  248.3 2.1 multiply_reduce_fusion.1
  250.4 2.0 divide_reduce_fusion
  252.7 2.0 fusion.70
  254.7 1.2 convolution_convert_fusion
  256.0 1.2 copy.20
  257.1 2.6 slice_bitcast_fusion
  259.8 67.1 %all-gather.7.cloned.1.call-done = f32[32,641,72]{1,2,0:T(8,128)} async-done(((f32[1,641,72]{1,2,0:T(8,128)}), f32[32,641,72]{1,2,0:T(8,128)}) %all-gather.7.cloned.1.call-update) | async-done | bytes 5907472 | tf_op jit(solution)/shard_map/all_gather | solution.py:80
  326.9 4.1 %reduce_sum.59 = f32[641,72]{0,1:T(8,128)} reduce(f32[32,641,72]{1,2,0:T(8,128)} %all-gather.7.cloned.1.call-done, f32[]{:T(128)} %constant.38.clone.1), dimensions={0}, to_apply=%region_5.6 | reduce | flops 1430712 | bytes 6092068 | tf_op jit(solution)/shard_map/reduce_sum | solution.py:81
  (48 shorter events, 5.3 us)
Async XLA Ops:
  7.2 165.9 %copy-start = (bf16[641,1282]{1,0:T(8,128)(2,1)S(1)}, bf16[641,1282]{1,0:T(8,128)(2,1)}, u32[]{:S(2)}) copy-start(bf16[641,1282]{1,0:T(8,128)(2,1)} %param.9) | copy-start | bytes 4930576
  7.2 241.1 %all-gather.5.cloned.1.call-start = ((), (), s32[]{:S(2)}) async-start(), calls=%async_computation | async-start | bytes 2211840 | tf_op jit(solution)/shard_map/all_gather | solution.py:64
  9.6 15.7 %collective-permute-start = (bf16[1,641,2,128]{3,1,2,0:T(8,128)(2,1)S(1)}, bf16[1,641,2,128]{3,1,2,0:T(8,128)(2,1)S(1)}, u32[]{:S(2)}, u32[]{:S(2)}) collective-permute-start(bf16[1,641,2,128]{3,1,2,0:T(8,128)(2,1)S(1)} %copy.13), channel_id=1, source_target_pairs={{0,1},{1,2},{2,3},{3,4},{4,5},{5,6},{6,7},{7,0},{8,9},{9,10},{10,1... | collective-permute-start | bytes 984584 | tf_op jit(solution)/shard_map/ppermute | solution.py:17
  11.3 16.0 %collective-permute-start.1 = (bf16[1,641,2,128]{3,1,2,0:T(8,128)(2,1)S(1)}, bf16[1,641,2,128]{3,1,2,0:T(8,128)(2,1)S(1)}, u32[]{:S(2)}, u32[]{:S(2)}) collective-permute-start(bf16[1,641,2,128]{3,1,2,0:T(8,128)(2,1)S(1)} %copy.14), channel_id=1, source_target_pairs={{1,0},{2,1},{3,2},{4,3},{5,4},{6,5},{7,6},{0,7},{9,8},{10,9},{11,1... | collective-permute-start | bytes 984584 | tf_op jit(solution)/shard_map/ppermute | solution.py:19
  15.9 5.0 %copy-start.8 = (f32[641,5,5]{0,2,1:T(8,128)S(1)}, f32[641,5,5]{0,2,1:T(8,128)}, u32[]{:S(2)}) copy-start(f32[641,5,5]{0,2,1:T(8,128)} %param.8) | copy-start | bytes 192304
  15.9 11.6 %copy-start.5 = (bf16[1,641,24,128]{3,2,1,0:T(8,128)(2,1)S(1)}, bf16[1,641,24,128]{3,2,1,0:T(8,128)(2,1)}, u32[]{:S(2)}) copy-start(bf16[1,641,24,128]{3,2,1,0:T(8,128)(2,1)} %param.7) | copy-start | bytes 11814916
  164.9 5.5 %copy-start.2 = (f32[1,641,24,128]{3,2,1,0:T(8,128)S(1)}, f32[1,641,24,128]{3,2,1,0:T(8,128)}, u32[]{:S(2)}) copy-start(f32[1,641,24,128]{3,2,1,0:T(8,128)} %get-tuple-element.28) | copy-start | bytes 23629828
  171.9 44.2 %slice-start = ((s8[7962624]{0:T(1024)(128)(4,1)}), s8[4194304]{0:T(1024)(128)(4,1)S(1)}, s32[]{:S(2)}) async-start(s8[7962624]{0:T(1024)(128)(4,1)} %bitcast.138), calls=%async_computation.2 | async-start | bytes 8388608
  173.1 43.0 %slice-start.1 = ((s8[7962624]{0:T(1024)(128)(4,1)}), s8[3768320]{0:T(1024)(128)(4,1)S(1)}, s32[]{:S(2)}) async-start(s8[7962624]{0:T(1024)(128)(4,1)} %bitcast.138), calls=%async_computation.3 | async-start | bytes 7536640
  173.1 43.0 %copy-start.10 = (bf16[1282,641]{0,1:T(8,128)(2,1)S(1)}, bf16[1282,641]{0,1:T(8,128)(2,1)}, u32[]{:S(2)}) copy-start(bf16[1282,641]{0,1:T(8,128)(2,1)} %param.10) | copy-start | bytes 4930576
  216.1 9.1 %copy-start.7 = (bf16[641,72]{0,1:T(8,128)(2,1)S(1)}, bf16[641,72]{0,1:T(8,128)(2,1)}, u32[]{:S(2)}) copy-start(bf16[641,72]{0,1:T(8,128)(2,1)} %param.11) | copy-start | bytes 276916
  223.4 1.9 copy-start.3
  225.2 1.9 copy-start.6
  225.2 2.1 copy-start.9
  226.9 100.0 %all-gather.7.cloned.1.call-start = ((), (), s32[]{:S(2)}) async-start(), calls=%async_computation.1 | async-start | bytes 7299072 | tf_op jit(solution)/shard_map/all_gather | solution.py:80
  248.3 4.4 %copy-start.4 = (bf16[641,3072]{1,0:T(8,128)(2,1)S(1)}, bf16[641,3072]{1,0:T(8,128)(2,1)}, u32[]{:S(2)}) copy-start(bf16[641,3072]{1,0:T(8,128)(2,1)} %copy-done.3) | copy-start | bytes 11814916
  256.0 75.0 %copy-start.1 = (bf16[641,1282]{1,0:T(8,128)(2,1)S(1)}, bf16[641,1282]{1,0:T(8,128)(2,1)}, u32[]{:S(2)}) copy-start(bf16[641,1282]{1,0:T(8,128)(2,1)} %param.9) | copy-start | bytes 4930576
Sparse Core Ops, SparseCore 0:
  227.0 21.2 all-gather.4
  254.9 71.9 all-gather.6
